TPU v7x, 32 devices: a whole 2x2x4 slice. The times are simulated.
32 devices in a mesh: row: 16 (over z, y, core), col: 2 (over x).
Axes of the slice: x: 2, y: 2, z: 4, core: 2. Of those that a mesh axis runs over, the one named last changes fastest.
Arguments:
- slab: bfloat16 [4096, 4096], P('row', 'col'), may hold values from -6 to 6
- slab_mask: int32 [32, 32], P('row', 'col'), may hold values 0 or 1
- density: bfloat16 [4096, 4096], P('row', 'col'), may hold values from -0.125 to 0.125
- block_mask: int32 [32, 32], P('row', 'col'), may hold values 0 or 1
Outputs:
- purified: bfloat16 [4096, 4096], P('row', 'col')
Inputs may be any that keep to these rules, and one draw needn't show every extreme that they name: `slab_mask`: 0 or 1 per block. `block_mask`: 0 or 1 per block.
All inputs are finite; a program needn't handle non-finite values.
Results may differ from a plain program's by a relative error of at most 0.005.
Values may be sent and summed in bfloat16 or wider, within the bound.
A program may use at most 64 MiB of HBM per device.

v0:
```python
import jax
import jax.numpy as jnp
from jax import lax
from jax.sharding import PartitionSpec as P


def expand(mask, block):
    height, width = mask.shape
    spread = jnp.broadcast_to(mask[:, None, :, None], (height, block, width, block))
    return spread.reshape(height * block, width * block)


def per_device(slab, slab_mask, density, block_mask):
    block = density.shape[0] // block_mask.shape[0]
    dense = density * expand(block_mask, block).astype(jnp.bfloat16)
    rows = slab * expand(slab_mask, block).astype(jnp.bfloat16)
    row_panel = lax.all_gather(rows, "col", axis=1, tiled=True)
    column = lax.all_gather(dense, "row", axis=0, tiled=True)
    square = jnp.dot(row_panel, column, preferred_element_type=jnp.float32).astype(jnp.bfloat16)
    square_rows = lax.all_gather(square, "col", axis=1, tiled=True)
    cube = jnp.dot(square_rows, column, preferred_element_type=jnp.float32)
    return (3.0 * square.astype(jnp.float32) - 2.0 * cube).astype(jnp.bfloat16)


def solution(mesh):
    placed = (P("row", "col"), P("row", "col"), P("row", "col"), P("row", "col"))
    return jax.shard_map(
        per_device, mesh=mesh, in_specs=placed, out_specs=P("row", "col"), check_vma=False
    )
```

profile of v0, /device:TPU:1, one launch (start us, length us, event | category | flops | bytes accessed | tf_op | source)
XLA Modules:
  0.0 235.7 jit_solution(9267352462086126830)
XLA Ops:
  6.5 0.0 all-gather.4.cloned.1.call-start
  6.5 0.7 convert_element_type.23
  7.2 0.2 broadcast_in_dim.4
  7.4 0.0 copy-start.1
  7.4 0.0 copy-start
  7.5 2.5 %bitcast_multiply_fusion.1 = bf16[256,2048]{1,0:T(8,128)(2,1)} fusion(bf16[256,2048]{1,0:T(8,128)(2,1)} %param.4, bf16[32,8,16,128]{3,2,1,0:T(8,128)(2,1)S(1)} %bitcast.12), kind=kLoop, calls=%fused_computation.5 | loop fusion | flops 524288 | bytes 3145728 | tf_op jit(solution)/shard_map/mul | solution.py:16
  10.0 0.0 all-gather.4.cloned.1.call-update
  10.0 0.0 all-gather.6.cloned.1.call-start
  10.1 0.0 copy-done.1
  10.1 0.2 broadcast_in_dim.5
  10.3 0.0 copy-done
  10.3 1.2 bitcast_multiply_fusion
  11.5 0.0 all-gather.6.cloned.1.call-update
  11.5 0.0 all-gather.8.cloned.1.call-start
  11.6 33.6 %all-gather.4.cloned.1.call-done = bf16[256,4096]{1,0:T(8,128)(2,1)} async-done(((bf16[256,2048]{1,0:T(8,128)(2,1)}), bf16[256,4096]{1,0:T(8,128)(2,1)}) %all-gather.4.cloned.1.call-update) | async-done | bytes 2097168 | tf_op jit(solution)/shard_map/all_gather | solution.py:17
  45.1 129.2 %all-gather.6.cloned.1.call-done = bf16[4096,2048]{1,0:T(8,128)(2,1)} async-done(((bf16[256,2048]{1,0:T(8,128)(2,1)}), bf16[4096,2048]{1,0:T(8,128)(2,1)}) %all-gather.6.cloned.1.call-update) | async-done | bytes 16777232 | tf_op jit(solution)/shard_map/all_gather | solution.py:18
  174.4 11.9 %convolution_convert_fusion = bf16[256,2048]{1,0:T(8,128)(2,1)} fusion(bf16[256,4096]{1,0:T(8,128)(2,1)} %all-gather.4.cloned.1.call-done, bf16[4096,2048]{1,0:T(8,128)(2,1)} %all-gather.6.cloned.1.call-done), kind=kOutput, calls=%fused_computation.3 | convolution fusion | flops 4295491584 | bytes 19922944 | tf_op jit(solution)/shard_map/dot_general | solution.py:19
  186.2 0.0 all-gather.8.cloned.1.call-update
  186.2 30.8 %all-gather.8.cloned.1.call-done = bf16[256,4096]{1,0:T(8,128)(2,1)} async-done(((bf16[256,2048]{1,0:T(8,128)(2,1)}), bf16[256,4096]{1,0:T(8,128)(2,1)}) %all-gather.8.cloned.1.call-update) | async-done | bytes 2097168 | tf_op jit(solution)/shard_map/all_gather | solution.py:20
  217.1 12.1 %fusion.1 = bf16[256,2048]{1,0:T(8,128)(2,1)} fusion(bf16[256,4096]{1,0:T(8,128)(2,1)} %all-gather.8.cloned.1.call-done, bf16[4096,2048]{1,0:T(8,128)(2,1)} %all-gather.6.cloned.1.call-done, bf16[256,2048]{1,0:T(8,128)(2,1)} %convolution_convert_fusion), kind=kOutput, calls=%fused_computation.2 | convolution fusion | flops 4297588736 | bytes 20971520 | tf_op jit(solution)/shard_map/dot_general | solution.py:21
  (1 shorter events, 0.0 us)
Async XLA Ops:
  6.5 38.6 %all-gather.4.cloned.1.call-start = ((), (), s32[]{:S(2)}) async-start(), calls=%async_computation | async-start | bytes 3145728 | tf_op jit(solution)/shard_map/all_gather | solution.py:17
  7.4 2.6 %copy-start.1 = (s32[2,16]{1,0:T(2,128)S(1)}, s32[2,16]{1,0:T(2,128)}, u32[]{:S(2)}) copy-start(s32[2,16]{1,0:T(2,128)} %param.7) | copy-start | bytes 388
  7.4 2.8 %copy-start = (bf16[256,2048]{1,0:T(8,128)(2,1)S(1)}, bf16[256,2048]{1,0:T(8,128)(2,1)}, u32[]{:S(2)}) copy-start(bf16[256,2048]{1,0:T(8,128)(2,1)} %param.6) | copy-start | bytes 3145732
  10.0 164.4 %all-gather.6.cloned.1.call-start = ((), (), s32[]{:S(2)}) async-start(), calls=%async_computation.1 | async-start | bytes 17825792 | tf_op jit(solution)/shard_map/all_gather | solution.py:18
  11.5 205.5 %all-gather.8.cloned.1.call-start = ((), (), s32[]{:S(2)}) async-start(), calls=%async_computation.2 | async-start | bytes 3145728 | tf_op jit(solution)/shard_map/all_gather | solution.py:20
Sparse Core Ops, SparseCore 0:
  10.1 34.9 all-gather.3
  47.3 127.0 all-gather.5
  186.4 30.6 all-gather.7
where the time goes:
time: 237 us; the launch traced here: 236 us
  waiting for transfers between devices  194 us (82%)
  matrix products  23.9 us (10%)
  between operations  13.2 us (6%)
  other arithmetic  4.43 us (2%)
    all_gather x1, waiting for transfers between devices, per_device(): column = lax.all_gather(dense, 'row', axis=0, tiled=True)  129 us
    all_gather x1, waiting for transfers between devices, per_device(): row_panel = lax.all_gather(rows, 'col', axis=1, tiled=True)  33.6 us
    all_gather x1, waiting for transfers between devices, per_device(): square_rows = lax.all_gather(square, 'col', axis=1, tiled=True)  30.8 us
    dot_general x1, matrix products, per_device(): cube = jnp.dot(square_rows, column, preferred_element_type=jnp.float32)  12.1 us
    dot_general x1, matrix products, per_device(): jnp.dot(row_panel, column, preferred_element_type=jnp.float32)  11.9 us
  transfers between devices with their start and end apart: 3, of which 3 were waited for; matrix products, arithmetic and copies ran while one was open for 1% of the time, Pallas kernels for 0%

commit v1 on v0

v1 whole, which is shorter than its diff:
```python
import functools

import jax
import jax.numpy as jnp
from jax import lax
from jax.experimental import pallas as pl
from jax.experimental.pallas import tpu as pltpu
from jax.sharding import PartitionSpec as P

MESH = pl.DeviceIdType.MESH
CHUNKS = 4


def kernel(nrow, ncol, slab, slab_mask, density, block_mask, out,
           panel, rows, square, cube, up_s, dn_s, y_s, core_s, arrive, arrive_half,
           rows_s, rows_r, sq_s, sq_r):
    height, cols = density.shape
    block = height // block_mask.shape[0]
    half = height // 2
    width = panel.shape[2]
    nchunk = panel.shape[0]
    kblock = rows.shape[2]
    per = cols // kblock
    Z = nrow // 4
    me = lax.axis_index("row")
    mc = lax.axis_index("col")
    z, y, c = me // 4, lax.rem(me // 2, 2), lax.rem(me, 2)
    flip_z = z + 1 - 2 * lax.rem(z, 2)
    flip_y = 1 - y
    up, dn = me + 4, me - 4
    over_y = me + 2 - 4 * y
    over_c = me + 1 - 2 * c
    over_z = me + 4 - 8 * lax.rem(z, 2)

    def row_of(zz, yy, cc):
        return (zz * 2 + yy) * 2 + cc

    for i in range(height // block):
        for k in range(cols // block):
            at_row, at_col = i * block, k * block
            keep = jnp.full((block, block), block_mask[i, k], jnp.int32).astype(jnp.float32).astype(jnp.bfloat16)
            start = pl.multiple_of(me * height + at_row, block)
            panel[at_col // width, pl.ds(start, block), at_col % width:at_col % width + block] = (
                density[at_row:at_row + block, at_col:at_col + block] * keep)
    for i in range(height // block):
        for k in range(cols // block):
            at_row, at_col = i * block, k * block
            keep = jnp.full((block, block), slab_mask[i, k], jnp.int32).astype(jnp.float32).astype(jnp.bfloat16)
            rows[mc * per + at_col // kblock, at_row:at_row + block, at_col % kblock:at_col % kblock + block] = (
                slab[at_row:at_row + block, at_col:at_col + block] * keep)

    barrier = pltpu.get_barrier_semaphore()

    def greet(row):
        pl.semaphore_signal(barrier, inc=1, device_id={"row": row}, device_id_type=MESH)

    pl.when(z < Z - 1)(lambda: greet(up))
    pl.when(z > 0)(lambda: greet(dn))
    greet(over_y)
    greet(over_c)
    for d in range(1, ncol):
        pl.semaphore_signal(barrier, inc=1, device_id={"col": lax.rem(mc + d, ncol)}, device_id_type=MESH)
    pl.semaphore_wait(barrier, (z < Z - 1).astype(jnp.int32) + (z > 0).astype(jnp.int32) + 1 + ncol)

    def copy(j, source, first, count, send, recv, target):
        ref = panel.at[j, pl.ds(pl.multiple_of(source * height + first, half), count), :]
        return pltpu.make_async_remote_copy(
            src_ref=ref, dst_ref=ref, send_sem=send, recv_sem=recv,
            device_id={"row": target}, device_id_type=MESH)

    def full(j, source, send, target):
        return copy(j, source, 0, height, send, arrive.at[j, source], target)

    def top(j, source, send, target):
        return copy(j, source, 0, half, send, arrive.at[j, source], target)

    def to_up(j, zz):
        return full(j, row_of(zz, y, c), up_s.at[j, zz], up)

    def to_dn(j, zz):
        return full(j, row_of(zz, y, c), dn_s.at[j, zz], dn)

    def to_y(j, zz):
        return full(j, row_of(zz, y, c), y_s.at[j, zz], over_y)

    def to_y_top(j, zz):
        return top(j, row_of(zz, y, c), y_s.at[j, zz], over_y)

    def to_core(j, zz, yy):
        return full(j, row_of(zz, yy, c), core_s.at[j, zz * 2 + yy], over_c)

    def to_z_half(j):
        return copy(j, row_of(z, flip_y, c), half, half, up_s.at[j, Z], arrive_half.at[j], over_z)

    def got_full(j, source):
        full(j, source, up_s.at[j, 0], over_c).wait_recv()

    def got_top(j, source):
        top(j, source, up_s.at[j, 0], over_c).wait_recv()

    def got_z_half(j):
        copy(j, row_of(flip_z, flip_y, c), half, half, up_s.at[j, Z], arrive_half.at[j], over_z).wait_recv()

    def send_own(j):
        pl.when(z < Z - 1)(lambda: to_up(j, z).start())
        pl.when(z > 0)(lambda: to_dn(j, z).start())
        to_y(j, z).start()
        to_core(j, z, y).start()

    def pass_y(j, zz, act):
        pl.when(zz == flip_z)(lambda: act(to_y_top(j, zz)))
        pl.when(zz != flip_z)(lambda: act(to_y(j, zz)))

    start = lambda cp: cp.start()
    finish = lambda cp: cp.wait_send()

    def line(j):
        for s in range(1, Z):
            @pl.when(z >= s)
            def _():
                zz = z - s
                got_full(j, row_of(zz, y, c))
                pl.when(z < Z - 1)(lambda: to_up(j, zz).start())
                pass_y(j, zz, start)
                to_core(j, zz, y).start()

            @pl.when(z + s < Z)
            def _():
                zz = z + s
                got_full(j, row_of(zz, y, c))
                pl.when(z > 0)(lambda: to_dn(j, zz).start())
                pass_y(j, zz, start)
                to_core(j, zz, y).start()

            if s == 1:
                got_full(j, row_of(z, flip_y, c))
                to_z_half(j).start()
                to_core(j, z, flip_y).start()

    def others(j):
        got_top(j, row_of(flip_z, flip_y, c))
        got_z_half(j)
        to_core(j, flip_z, flip_y).start()

        def one(zz, _):
            @pl.when((zz != z) & (zz != flip_z))
            def _():
                got_full(j, row_of(zz, flip_y, c))
                to_core(j, zz, flip_y).start()
            return 0
        lax.fori_loop(0, Z, one, 0)

        def two(k, _):
            got_full(j, k * 2 + 1 - c)
            return 0
        lax.fori_loop(0, nrow // 2, two, 0)

    def rows_copy(d):
        ref = rows.at[pl.ds(mc * per, per)]
        return pltpu.make_async_remote_copy(
            src_ref=ref, dst_ref=ref, send_sem=rows_s.at[d], recv_sem=rows_r.at[mc],
            device_id={"col": lax.rem(mc + d, ncol)}, device_id_type=MESH)

    def rows_got(d):
        who = lax.rem(mc + d, ncol)
        ref = rows.at[pl.ds(who * per, per)]
        pltpu.make_async_remote_copy(
            src_ref=ref, dst_ref=ref, send_sem=rows_s.at[d], recv_sem=rows_r.at[who],
            device_id={"col": who}, device_id_type=MESH).wait_recv()

    def sq_copy(j, d):
        ref = square.at[mc * nchunk + j]
        return pltpu.make_async_remote_copy(
            src_ref=ref, dst_ref=ref, send_sem=sq_s.at[j, d], recv_sem=sq_r.at[j, mc],
            device_id={"col": lax.rem(mc + d, ncol)}, device_id_type=MESH)

    def sq_got(j, d):
        who = lax.rem(mc + d, ncol)
        ref = square.at[who * nchunk + j]
        pltpu.make_async_remote_copy(
            src_ref=ref, dst_ref=ref, send_sem=sq_s.at[j, d], recv_sem=sq_r.at[j, who],
            device_id={"col": who}, device_id_type=MESH).wait_recv()

    def make_square(j):
        cube[j] = jnp.zeros(cube.shape[1:], cube.dtype)

        def one(k, _):
            cube[j] += jnp.dot(rows[k], panel[j, pl.ds(pl.multiple_of(k * kblock, kblock), kblock), :],
                               preferred_element_type=jnp.float32)
            return 0
        lax.fori_loop(0, rows.shape[0], one, 0)
        square[mc * nchunk + j] = cube[j].astype(jnp.bfloat16)
        for d in range(1, ncol):
            sq_copy(j, d).start()

    send_own(0)
    for d in range(1, ncol):
        rows_copy(d).start()

    def chunk(t, _):
        pl.when(t + 1 < nchunk)(lambda: send_own(t + 1))
        pl.when(t < nchunk)(lambda: line(t))

        @pl.when(t == 1)
        def _():
            for d in range(1, ncol):
                rows_got(d)

        @pl.when(t >= 1)
        def _():
            others(t - 1)
            make_square(t - 1)
        return 0
    lax.fori_loop(0, nchunk + 1, chunk, 0)

    last = nchunk - 1

    def add(n, at):
        cube[n] += jnp.dot(square[at], panel[n, pl.ds(pl.multiple_of(at * width, width), width), :],
                           preferred_element_type=jnp.float32)

    def clear(n, _):
        cube[n] = jnp.zeros(cube.shape[1:], cube.dtype)
        return 0
    lax.fori_loop(0, nchunk, clear, 0)

    def early(k, _):
        for d in range(1, ncol):
            sq_got(k, d)

        def col(n, _):
            for d in range(ncol):
                add(n, lax.rem(mc + d, ncol) * nchunk + k)
            return 0
        lax.fori_loop(0, nchunk, col, 0)
        return 0
    lax.fori_loop(0, last, early, 0)

    def own(n, _):
        add(n, mc * nchunk + last)
        return 0
    lax.fori_loop(0, nchunk, own, 0)
    for d in range(1, ncol):
        sq_got(last, d)

    def final(n, _):
        for d in range(1, ncol):
            add(n, lax.rem(mc + d, ncol) * nchunk + last)
        out[:, pl.ds(pl.multiple_of(n * width, width), width)] = (
            3.0 * square[mc * nchunk + n].astype(jnp.float32) - 2.0 * cube[n]).astype(out.dtype)
        return 0
    lax.fori_loop(0, nchunk, final, 0)

    def drain(j, _):
        def one(zz, _):
            pl.when((z < Z - 1) & (zz <= z))(lambda: to_up(j, zz).wait_send())
            pl.when((z > 0) & (zz >= z))(lambda: to_dn(j, zz).wait_send())
            pass_y(j, zz, finish)
            to_core(j, zz, y).wait_send()
            to_core(j, zz, flip_y).wait_send()
            return 0
        lax.fori_loop(0, Z, one, 0)
        to_z_half(j).wait_send()
        for d in range(1, ncol):
            sq_copy(j, d).wait_send()
        return 0
    lax.fori_loop(0, nchunk, drain, 0)
    for d in range(1, ncol):
        rows_copy(d).wait_send()


def per_device(nrow, ncol, slab, slab_mask, density, block_mask):
    height, cols = density.shape
    tall = slab.shape[0]
    width = cols // CHUNKS
    zs = nrow // 4
    kblock = cols // 2
    vmem = pl.BlockSpec(memory_space=pltpu.VMEM)
    smem = pl.BlockSpec(memory_space=pltpu.SMEM)
    dma = pltpu.SemaphoreType.DMA
    return pl.pallas_call(
        functools.partial(kernel, nrow, ncol),
        out_shape=jax.ShapeDtypeStruct((tall, cols), jnp.bfloat16),
        in_specs=[vmem, smem, vmem, smem],
        out_specs=vmem,
        scratch_shapes=[
            pltpu.VMEM((CHUNKS, height * nrow, width), jnp.bfloat16),
            pltpu.VMEM((ncol * cols // kblock, tall, kblock), jnp.bfloat16),
            pltpu.VMEM((ncol * CHUNKS, tall, width), jnp.bfloat16),
            pltpu.VMEM((CHUNKS, tall, width), jnp.float32),
            dma((CHUNKS, zs + 1)), dma((CHUNKS, zs)), dma((CHUNKS, zs)), dma((CHUNKS, 2 * zs)),
            dma((CHUNKS, nrow)), dma((CHUNKS,)),
            dma((ncol,)), dma((ncol,)), dma((CHUNKS, ncol)), dma((CHUNKS, ncol)),
        ],
        compiler_params=pltpu.CompilerParams(
            collective_id=0, has_side_effects=True, vmem_limit_bytes=48 * 1024 * 1024),
    )(slab, slab_mask, density, block_mask)


def solution(mesh):
    placed = (P("row", "col"), P("row", "col"), P("row", "col"), P("row", "col"))
    return jax.shard_map(
        functools.partial(per_device, mesh.shape["row"], mesh.shape["col"]),
        mesh=mesh, in_specs=placed, out_specs=P("row", "col"), check_vma=False
    )
```

time: 237 us -> 110 us (0.46)
  waiting for transfers between devices: 194 us -> 0 us
  Pallas kernels: 0 us -> 105 us
  matrix products: 23.9 us -> 0 us
  between operations: 13.2 us -> 0.01 us
  other arithmetic: 4.43 us -> 0 us
  local copies, waits for them, and re-layouts: 0.42 us -> 4.78 us
    all_gather x3 -> x0, waiting for transfers between devices: 194 us -> none  [the longest x1 129 us: per_device(): column = lax.all_gather(dense, 'row', axis=0, tiled=True)]
    pallas_call x0 -> x1, Pallas kernels: none -> 105 us  [per_device(): pl.pallas_call(functools.partial(kernel, nrow, ncol), out_shape=jax.Shape...]
    dot_general x2 -> x0, matrix products: 23.9 us -> none  [the longest x1 12.1 us: per_device(): cube = jnp.dot(square_rows, column, preferred_element_type=jnp.float32)]
    unnamed x4 -> x9, local copies, waits for them, and re-layouts: 0.01 us -> 4.78 us
    mul x2 -> x0, other arithmetic: 3.75 us -> none  [the longest x1 2.52 us: per_device(): rows = slab * expand(slab_mask, block).astype(jnp.bfloat16)]
  transfers between devices with their start and end apart: 3 -> 0, of which waited for: 3 -> 0; matrix products, arithmetic and copies ran while one was open for 1% -> 0% of each run, Pallas kernels for 0% -> 0%
where the time goes in v1:
time: 110 us
  Pallas kernels  105 us (95%)
  local copies, waits for them, and re-layouts  4.78 us (4%)
    pallas_call x1, Pallas kernels, per_device(): pl.pallas_call(functools.partial(kernel, nrow, ncol), out_shape=jax.Shape...  105 us
    unnamed x9, local copies, waits for them, and re-layouts  4.78 us

profile of v1, /device:TPU:1, one launch (start us, length us, event | category | flops | bytes accessed | tf_op | source)
XLA Modules:
  0.0 109.5 jit_solution(3929510135004861656)
XLA Ops:
  0.0 0.0 copy-start
  0.0 1.2 %copy-done = bf16[256,2048]{1,0:T(8,128)(2,1)S(1)} copy-done((bf16[256,2048]{1,0:T(8,128)(2,1)S(1)}, bf16[256,2048]{1,0:T(8,128)(2,1)}, u32[]{:S(2)}) %copy-start) | copy-done | bytes 1048600
  1.2 0.0 copy-start.1
  1.2 1.2 %copy-done.1 = bf16[256,2048]{1,0:T(8,128)(2,1)S(1)} copy-done((bf16[256,2048]{1,0:T(8,128)(2,1)S(1)}, bf16[256,2048]{1,0:T(8,128)(2,1)}, u32[]{:S(2)}) %copy-start.1) | copy-done | bytes 1048600
  2.5 0.0 copy-start.2
  2.5 0.7 copy-done.2
  3.1 0.0 copy-start.3
  3.1 0.7 copy-done.3
  3.8 104.8 %shard_map.46 = bf16[256,2048]{1,0:T(8,128)(2,1)S(1)} custom-call(bf16[256,2048]{1,0:T(8,128)(2,1)S(1)} %copy-done, s32[2,16]{1,0:T(2,128)S(1)} %copy-done.2, bf16[256,2048]{1,0:T(8,128)(2,1)S(1)} %copy-done.1, s32[2,16]{1,0:T(2,128)S(1)} %copy-done.3), custom_call_target="tpu_custom_call" | custom-call | tf_op jit(solution)/shard_map/pallas_call | solution.py:281
  108.6 1.0 copy.6
Async XLA Ops:
  0.0 1.2 %copy-start = (bf16[256,2048]{1,0:T(8,128)(2,1)S(1)}, bf16[256,2048]{1,0:T(8,128)(2,1)}, u32[]{:S(2)}) copy-start(bf16[256,2048]{1,0:T(8,128)(2,1)} %slab.1) | copy-start | bytes 3145732
  1.2 1.2 %copy-start.1 = (bf16[256,2048]{1,0:T(8,128)(2,1)S(1)}, bf16[256,2048]{1,0:T(8,128)(2,1)}, u32[]{:S(2)}) copy-start(bf16[256,2048]{1,0:T(8,128)(2,1)} %density.1) | copy-start | bytes 3145732
  2.5 0.7 copy-start.2
  3.1 0.7 copy-start.3

commit v2 on v1

--- a/solution.py
+++ b/solution.py
@@ -182,14 +182,11 @@
             device_id={"col": who}, device_id_type=MESH).wait_recv()
 
     def make_square(j):
-        cube[j] = jnp.zeros(cube.shape[1:], cube.dtype)
-
-        def one(k, _):
-            cube[j] += jnp.dot(rows[k], panel[j, pl.ds(pl.multiple_of(k * kblock, kblock), kblock), :],
-                               preferred_element_type=jnp.float32)
-            return 0
-        lax.fori_loop(0, rows.shape[0], one, 0)
-        square[mc * nchunk + j] = cube[j].astype(jnp.bfloat16)
+        whole = None
+        for k in range(rows.shape[0]):
+            part = jnp.dot(rows[k], panel[j, k * kblock:(k + 1) * kblock, :], preferred_element_type=jnp.float32)
+            whole = part if whole is None else whole + part
+        square[mc * nchunk + j] = whole.astype(jnp.bfloat16)
         for d in range(1, ncol):
             sq_copy(j, d).start()
 
@@ -215,39 +212,31 @@
 
     last = nchunk - 1
 
-    def add(n, at):
-        cube[n] += jnp.dot(square[at], panel[n, pl.ds(pl.multiple_of(at * width, width), width), :],
-                           preferred_element_type=jnp.float32)
-
-    def clear(n, _):
-        cube[n] = jnp.zeros(cube.shape[1:], cube.dtype)
-        return 0
-    lax.fori_loop(0, nchunk, clear, 0)
-
-    def early(k, _):
+    def term(n, at):
+        return jnp.dot(square[at], panel[n, pl.ds(pl.multiple_of(at * width, width), width), :],
+                       preferred_element_type=jnp.float32)
+
+    for k in range(last):
         for d in range(1, ncol):
             sq_got(k, d)
 
-        def col(n, _):
+    def early(n, _):
+        whole = term(n, mc * nchunk + last)
+        for k in range(last):
             for d in range(ncol):
-                add(n, lax.rem(mc + d, ncol) * nchunk + k)
-            return 0
-        lax.fori_loop(0, nchunk, col, 0)
-        return 0
-    lax.fori_loop(0, last, early, 0)
-
-    def own(n, _):
-        add(n, mc * nchunk + last)
-        return 0
-    lax.fori_loop(0, nchunk, own, 0)
+                whole = whole + term(n, lax.rem(mc + d, ncol) * nchunk + k)
+        cube[n] = whole
+        return 0
+    lax.fori_loop(0, nchunk, early, 0)
     for d in range(1, ncol):
         sq_got(last, d)
 
     def final(n, _):
-        for d in range(1, ncol):
-            add(n, lax.rem(mc + d, ncol) * nchunk + last)
+        whole = cube[n]
+        for d in range(1, ncol):
+            whole = whole + term(n, lax.rem(mc + d, ncol) * nchunk + last)
         out[:, pl.ds(pl.multiple_of(n * width, width), width)] = (
-            3.0 * square[mc * nchunk + n].astype(jnp.float32) - 2.0 * cube[n]).astype(out.dtype)
+            3.0 * square[mc * nchunk + n].astype(jnp.float32) - 2.0 * whole).astype(out.dtype)
         return 0
     lax.fori_loop(0, nchunk, final, 0)
 

time: 110 us -> 109 us (level)
  no operation moved by 1% of the time
where the time goes in v2:
time: 109 us
  Pallas kernels  104 us (95%)
  local copies, waits for them, and re-layouts  4.78 us (4%)
    pallas_call x1, Pallas kernels, per_device(): pl.pallas_call(functools.partial(kernel, nrow, ncol), out_shape=jax.Shape...  104 us
    unnamed x9, local copies, waits for them, and re-layouts  4.78 us

profile of v2, /device:TPU:1, one launch (start us, length us, event | category | flops | bytes accessed | tf_op | source)
XLA Modules:
  0.0 109.0 jit_solution(6870823547633029066)
XLA Ops:
  0.0 0.0 copy-start
  0.0 1.2 %copy-done = bf16[256,2048]{1,0:T(8,128)(2,1)S(1)} copy-done((bf16[256,2048]{1,0:T(8,128)(2,1)S(1)}, bf16[256,2048]{1,0:T(8,128)(2,1)}, u32[]{:S(2)}) %copy-start) | copy-done | bytes 1048600
  1.2 0.0 copy-start.1
  1.2 1.2 %copy-done.1 = bf16[256,2048]{1,0:T(8,128)(2,1)S(1)} copy-done((bf16[256,2048]{1,0:T(8,128)(2,1)S(1)}, bf16[256,2048]{1,0:T(8,128)(2,1)}, u32[]{:S(2)}) %copy-start.1) | copy-done | bytes 1048600
  2.5 0.0 copy-start.2
  2.5 0.7 copy-done.2
  3.1 0.0 copy-start.3
  3.1 0.7 copy-done.3
  3.8 104.2 %shard_map.46 = bf16[256,2048]{1,0:T(8,128)(2,1)S(1)} custom-call(bf16[256,2048]{1,0:T(8,128)(2,1)S(1)} %copy-done, s32[2,16]{1,0:T(2,128)S(1)} %copy-done.2, bf16[256,2048]{1,0:T(8,128)(2,1)S(1)} %copy-done.1, s32[2,16]{1,0:T(2,128)S(1)} %copy-done.3), custom_call_target="tpu_custom_call" | custom-call | tf_op jit(solution)/shard_map/pallas_call | solution.py:270
  108.0 1.0 copy.6
Async XLA Ops:
  0.0 1.2 %copy-start = (bf16[256,2048]{1,0:T(8,128)(2,1)S(1)}, bf16[256,2048]{1,0:T(8,128)(2,1)}, u32[]{:S(2)}) copy-start(bf16[256,2048]{1,0:T(8,128)(2,1)} %slab.1) | copy-start | bytes 3145732
  1.2 1.2 %copy-start.1 = (bf16[256,2048]{1,0:T(8,128)(2,1)S(1)}, bf16[256,2048]{1,0:T(8,128)(2,1)}, u32[]{:S(2)}) copy-start(bf16[256,2048]{1,0:T(8,128)(2,1)} %density.1) | copy-start | bytes 3145732
  2.5 0.7 copy-start.2
  3.1 0.7 copy-start.3
